TPU v7x, 32 devices: a whole 2x2x4 slice. The times are simulated.
32 devices in a mesh: rec: 8 (over z, core), frame: 4 (over y, x).
Axes of the slice: x: 2, y: 2, z: 4, core: 2. Of those that a mesh axis runs over, the one named last changes fastest.
Arguments:
- frames: bfloat16 [8, 6144, 256], P('rec', 'frame'), may hold values from -10 to 10
- texts: bfloat16 [16, 224, 256], P('rec', 'frame'), may hold values from -100 to 100
- pair_rec: int32 [16, 1], replicated, may hold values from 0 to 7, as said below
- pair_text: int32 [16], replicated, may hold values from 0 to 15, as said below
- pair_label: int32 [16], replicated, may hold values 0 or 1
Outputs:
- loss: float32 [], replicated
- grad_frames: bfloat16 [8, 6144, 256], P('rec', 'frame')
- grad_texts: bfloat16 [16, 224, 256], P('rec', 'frame')
Inputs may be any that keep to these rules, and one draw needn't show every extreme that they name: `pair_rec`: no recording is named by more than 6 pairs, some recording by exactly 6, and every recording by at least one. A pair's text is held by the index of rec one after, one before, or 4 after its recording (counted round): pair_text // 2 = (pair_rec + k) mod 8 with k one of 1, 7, 4.
All inputs are finite; a program needn't handle non-finite values.
Results may differ from a plain program's by a relative error of at most 0.0085.
Values may be sent and summed in bfloat16 or wider, within the bound.
No kernel may reach another device: no remote copies, remote signals or barrier semaphores. Data moves between devices by JAX's collectives and lax.ppermute only.
A program may use at most 64 MiB of HBM per device.

v0:
```python
import jax
import jax.numpy as jnp
from jax import lax
from jax.sharding import PartitionSpec as P

MOST = 6
EPS = 1e-06
TEMP = 10.0
BIAS = -1.0
LOSS_SCALE = 2048.0


def slot_tables(pair_rec, pair_text, pair_label, here, most):
    record = pair_rec[:, 0]
    count = record.shape[0]
    order = jnp.arange(count, dtype=jnp.int32)
    same = (record[:, None] == record[None, :]).astype(jnp.int32)
    earlier = (order[None, :] < order[:, None]).astype(jnp.int32)
    rank = jnp.sum(same * earlier, axis=1)
    places = jnp.arange(most, dtype=jnp.int32)
    chosen = ((record[None, :] == here) & (rank[None, :] == places[:, None])).astype(jnp.int32)
    valid = jnp.sum(chosen, axis=1)
    slot_text = jnp.sum(chosen * pair_text[None, :], axis=1)
    sign = jnp.sum(chosen * (2 * pair_label[None, :] - 1), axis=1)
    return (valid, slot_text, sign)


def pair_terms(score, valid, sign, tokens):
    margin = -sign * (TEMP * score + BIAS)
    loss_part = valid * jax.nn.softplus(margin)
    grad_cos = -LOSS_SCALE * TEMP * valid * sign * jax.nn.sigmoid(margin) / tokens
    return (loss_part, grad_cos)


def body(frames, texts, pair_rec, pair_text, pair_label):
    here = lax.axis_index("rec")
    part = lax.axis_index("frame")
    owned, width_rows, width = texts.shape
    tokens = width_rows * lax.axis_size("frame")
    n_text = owned * lax.axis_size("rec")
    valid, slot_text, sign = slot_tables(pair_rec, pair_text, pair_label, here, MOST)
    valid_f = valid.astype(jnp.float32)
    sign_f = sign.astype(jnp.float32)
    picks = (
        (slot_text[:, None] == jnp.arange(n_text, dtype=jnp.int32)[None, :]) & (valid[:, None] > 0)
    ).astype(jnp.bfloat16)
    local = jnp.einsum(
        "jc,cgx->jgx",
        picks,
        lax.all_gather(texts, "rec", axis=0, tiled=True),
        preferred_element_type=jnp.float32,
    ).astype(jnp.bfloat16)
    query_vectors = lax.all_gather(local, "frame", axis=1, tiled=True)
    upstream_signal = frames[0]
    logit_scale = width ** (-0.5)
    pair_scores = (
        jnp.einsum(
            "ype,je->ypj", query_vectors, upstream_signal, preferred_element_type=jnp.float32
        )
        * logit_scale
    )
    local_max = jnp.max(pair_scores, axis=2)
    row_max = lax.pmax(local_max, "frame")
    expo = jnp.exp(pair_scores - row_max[..., None])
    batch_weights = expo.astype(jnp.bfloat16)
    value_partial = jnp.einsum(
        "pqx,xh->pqh", batch_weights, upstream_signal, preferred_element_type=jnp.float32
    )
    query_f = query_vectors.astype(jnp.float32)
    q_norm = lax.rsqrt(jnp.sum(query_f * query_f, axis=2) + EPS)
    q_unit = query_f * q_norm[..., None]
    context = lax.psum(value_partial, "frame")
    c_norm = lax.rsqrt(jnp.sum(context * context, axis=2) + EPS)
    c_unit = context * c_norm[..., None]
    cos = jnp.sum(q_unit * c_unit, axis=2)
    score = jnp.mean(cos, axis=1)
    loss_part, grad_cos = pair_terms(score, valid_f, sign_f, tokens)
    weight = grad_cos[:, None, None]
    d_context = weight * (q_unit - cos[..., None] * c_unit) * c_norm[..., None]
    direct = weight * (c_unit - cos[..., None] * q_unit) * q_norm[..., None]
    direct_own = lax.dynamic_slice_in_dim(direct, part * width_rows, width_rows, 1)
    context_batch_gradient = d_context.astype(jnp.bfloat16)
    weight_gradient = jnp.einsum(
        "ype,je->ypj", context_batch_gradient, upstream_signal, preferred_element_type=jnp.float32
    )
    score_gradient = (expo * weight_gradient * logit_scale).astype(jnp.bfloat16)
    d_query = lax.psum_scatter(
        jnp.einsum(
            "slf,fd->lsd", score_gradient, upstream_signal, preferred_element_type=jnp.float32
        ),
        "frame",
        scatter_dimension=0,
        tiled=True,
    )
    d_query = d_query + jnp.transpose(direct_own, (1, 0, 2))
    text_term = jnp.einsum(
        "st,lsd->tld", picks.astype(jnp.float32), d_query, precision=lax.Precision.HIGHEST
    )
    grad_texts = lax.psum_scatter(text_term, "rec", scatter_dimension=0, tiled=True).astype(
        jnp.bfloat16
    )
    frame_loss_piece = jnp.einsum(
        "cvm,cvz->mz", score_gradient, query_vectors, preferred_element_type=jnp.float32
    )
    frame_loss_piece = frame_loss_piece + jnp.einsum(
        "cvm,cvz->mz", batch_weights, context_batch_gradient, preferred_element_type=jnp.float32
    )
    grad_frames = frame_loss_piece.astype(jnp.bfloat16)[None]
    loss = lax.psum(jnp.sum(loss_part), "rec")
    return (loss, grad_frames, grad_texts)


def solution(mesh):
    return jax.shard_map(
        body,
        mesh=mesh,
        in_specs=(P("rec", "frame", None), P("rec", "frame", None), P(), P(), P()),
        out_specs=(P(), P("rec", "frame", None), P("rec", "frame", None)),
        check_vma=False,
    )
```

profile of v0, /device:TPU:0, one launch (start us, length us, event | category | flops | bytes accessed | tf_op | source)
XLA Modules:
  0.0 205.2 jit_solution(4087020698551283832)
XLA Ops:
  7.2 0.7 multiply_add_fusion
  8.6 0.9 select_reduce_fusion
  9.5 0.8 select_reduce_fusion.2
  10.4 16.6 %all_gather.6 = bf16[16,56,256]{2,1,0:T(8,128)(2,1)S(1)} all-gather(bf16[2,56,256]{2,1,0:T(8,128)(2,1)} %param.6), channel_id=1, replica_groups=mesh['rec'=8,'frame'=4] {'rec'}, dimensions={0}, use_global_device_ids=true | all-gather | bytes 516096 | tf_op jit(solution)/shard_map/all_gather | solution.py:50
  27.3 12.4 %all_gather.7 = bf16[6,224,256]{2,1,0:T(8,128)(2,1)S(1)} all-gather(bf16[6,56,256]{2,1,0:T(8,128)(2,1)S(1)} %copy.20), channel_id=1, replica_groups=mesh['rec'=8,'frame'=4] {'frame'}, dimensions={1}, use_global_device_ids=true | all-gather | bytes 860160 | tf_op jit(solution)/shard_map/all_gather | solution.py:53
  39.7 4.4 %multiply_reduce_fusion = (f32[6,224]{1,0:T(8,128)S(1)}, f32[6,224,1536]{2,1,0:T(8,128)}) fusion(bf16[6,224,256]{2,1,0:T(8,128)(2,1)S(1)} %all_gather.7, bf16[1,1536,256]{2,1,0:T(8,128)(2,1)S(1)} %copy-done), kind=kOutput, calls=%fused_computation.2 | convolution fusion | flops 1061092032 | bytes 9737472 | tf_op jit(solution)/shard_map/ype,je->ypj/dot_general | solution.py:57
  44.1 9.1 %pmax.7 = f32[6,224]{1,0:T(8,128)S(1)} all-reduce(f32[6,224]{1,0:T(8,128)S(1)} %get-tuple-element.16), channel_id=1, replica_groups=mesh['rec'=8,'frame'=4] {'frame'}, use_global_device_ids=true, to_apply=%region_6.0 | all-reduce | flops 1344 | bytes 10752 | tf_op jit(solution)/shard_map/pmax | solution.py:63
  53.2 6.0 %fusion.7 = f32[6,224,256]{2,1,0:T(8,128)} fusion(bf16[1,1536,256]{2,1,0:T(8,128)(2,1)S(1)} %copy-done, f32[6,224,1536]{2,1,0:T(8,128)} %get-tuple-element.17, f32[6,224]{1,0:T(8,128)S(1)} %pmax.7), kind=kOutput, calls=%fused_computation.18 | convolution fusion | flops 1063157760 | bytes 10425600 | tf_op jit(solution)/shard_map/pqx,xh->pqh/dot_general | solution.py:66
  59.6 57.4 %all-reduce.2.cloned.1.call-done = f32[6,224,256]{2,1,0:T(8,128)} async-done(((f32[6,224,256]{2,1,0:T(8,128)}), f32[6,224,256]{2,1,0:T(8,128)}) %all-reduce.2.cloned.1.call-update) | async-done | bytes 1376272 | tf_op jit(solution)/shard_map/psum | solution.py:72
  116.9 1.8 multiply_reduce_fusion.1
  118.7 2.9 %multiply_reduce_fusion.2 = (f32[6,224]{1,0:T(8,128)S(1)}, f32[6]{0:T(128)S(1)}, f32[6,224,256]{2,1,0:T(8,128)S(1)}) fusion(f32[6,224]{1,0:T(8,128)S(1)} %add_rsqrt_fusion.1, bf16[6,224,256]{2,1,0:T(8,128)(2,1)S(1)} %all_gather.7, f32[6,224,256]{2,1,0:T(8,128)} %all-reduce.2.cloned.1.call-done, f32[6,224]{1,0:T(8,128)S(1)} %add_rsqrt_fusion), kind=kLoop, calls=%fused_computation.23 | loop fusion | flops 2063034 | bytes 3456792 | tf_op jit(solution)/shard_map/reduce_sum | solution.py:75
  122.3 1.6 convert_multiply_fusion
  123.9 2.3 %multiply_convert_fusion = bf16[6,224,1536]{2,1,0:T(8,128)(2,1)S(1)} fusion(f32[6,224,1536]{2,1,0:T(8,128)S(1)} %copy-done.1, bf16[6,224,256]{2,1,0:T(8,128)(2,1)S(1)} %get-tuple-element.13, f32[6,224]{1,0:T(8,128)S(1)} %copy-done.5, bf16[1,1536,256]{2,1,0:T(8,128)(2,1)S(1)} %copy-done), kind=kOutput, calls=%fused_computation | convolution fusion | flops 1067286528 | bytes 13866240 | tf_op jit(solution)/shard_map/ype,je->ypj/dot_general | solution.py:83
  126.2 2.0 copy-done.2
  128.2 2.3 %convolution_bitcast_fusion.2 = f32[224,6,256]{2,0,1:T(8,128)} fusion(bf16[6,224,1536]{2,1,0:T(8,128)(2,1)S(1)} %multiply_convert_fusion, bf16[1,1536,256]{2,1,0:T(8,128)(2,1)S(1)} %copy-done), kind=kOutput, calls=%fused_computation.11 | convolution fusion | flops 1056964608 | bytes 6291456 | tf_op jit(solution)/shard_map/slf,fd->lsd/dot_general | solution.py:88
  131.9 28.7 %reduce-scatter.3.cloned.1.call-done = f32[56,6,256]{2,0,1:T(8,128)} async-done(((f32[224,6,256]{2,0,1:T(8,128)}), f32[56,6,256]{2,0,1:T(8,128)}) %reduce-scatter.3.cloned.1.call-update) | async-done | bytes 344080 | tf_op jit(solution)/shard_map/reduce_scatter | solution.py:87
  160.5 1.2 fusion.19
  161.8 1.4 fusion.13
  163.2 1.5 copy.22
  164.7 17.1 %psum.15 = f32[]{:T(128)} all-reduce(f32[]{:T(128)} %get-tuple-element.15), channel_id=1, replica_groups=mesh['rec'=8,'frame'=4] {'rec'}, use_global_device_ids=true, to_apply=%region_11.12 | all-reduce | flops 1 | bytes 8 | tf_op jit(solution)/shard_map/psum | solution.py:109
  181.8 5.5 %convolution_bitcast_fusion = f32[1536,256]{1,0:T(8,128)S(1)} fusion(bf16[6,224,256]{2,1,0:T(8,128)(2,1)S(1)} %get-tuple-element.13, f32[6,224,1536]{2,1,0:T(8,128)} %get-tuple-element.17, f32[6,224]{1,0:T(8,128)S(1)} %copy-done.6), kind=kOutput, calls=%fused_computation.4 | convolution fusion | flops 1063157760 | bytes 10523904 | tf_op jit(solution)/shard_map/cvm,cvz->mz/dot_general | solution.py:105
  187.3 2.4 %fusion.3 = bf16[1,1536,256]{2,1,0:T(8,128)(2,1)} fusion(f32[1536,256]{1,0:T(8,128)S(1)} %convolution_bitcast_fusion, bf16[6,224,1536]{2,1,0:T(8,128)(2,1)S(1)} %copy-done.3, bf16[6,224,256]{2,1,0:T(8,128)(2,1)S(1)} %all_gather.7), kind=kOutput, calls=%fused_computation.8 | convolution fusion | flops 1057751040 | bytes 7176192 | tf_op jit(solution)/shard_map/cvm,cvz->mz/dot_general | solution.py:102
  189.7 7.5 %reduce-scatter.5.cloned.1.call-done = f32[2,56,256]{2,1,0:T(8,128)} async-done(((f32[16,56,256]{2,1,0:T(8,128)}), f32[2,56,256]{2,1,0:T(8,128)}) %reduce-scatter.5.cloned.1.call-update) | async-done | bytes 114704 | tf_op jit(solution)/shard_map/reduce_scatter | solution.py:99
  197.1 1.5 convert_element_type.54
  (35 shorter events, 3.4 us)
Async XLA Ops:
  7.2 32.5 %copy-start = (bf16[1,1536,256]{2,1,0:T(8,128)(2,1)S(1)}, bf16[1,1536,256]{2,1,0:T(8,128)(2,1)}, u32[]{:S(2)}) copy-start(bf16[1,1536,256]{2,1,0:T(8,128)(2,1)} %param.5) | copy-start | bytes 2359300
  7.2 109.8 %all-reduce.2.cloned.1.call-start = ((), (), s32[]{:S(2)}) async-start(), calls=%async_computation.2 | async-start | bytes 2752512 | tf_op jit(solution)/shard_map/psum | solution.py:72
  10.3 16.6 %copy-start.8 = (s32[6]{0:T(128)}, s32[6]{0:T(128)S(1)}, u32[]{:S(2)}) copy-start(s32[6]{0:T(128)S(1)} %get-tuple-element.9) | copy-start | bytes 76
  10.4 16.6 %copy-start.9 = (pred[6]{0:T(512)(128)(4,1)}, pred[6]{0:T(512)(128)(4,1)S(1)}, u32[]{:S(2)}) copy-start(pred[6]{0:T(512)(128)(4,1)S(1)} %broadcast_compare_fusion) | copy-start | bytes 22
  53.2 6.0 %copy-start.4 = (f32[6,224]{1,0:T(8,128)}, f32[6,224]{1,0:T(8,128)S(1)}, u32[]{:S(2)}) copy-start(f32[6,224]{1,0:T(8,128)S(1)} %pmax.7) | copy-start | bytes 16132
  59.2 101.3 %reduce-scatter.3.cloned.1.call-start = ((), (), s32[]{:S(2)}) async-start(), calls=%async_computation.3 | async-start | bytes 1720320 | tf_op jit(solution)/shard_map/reduce_scatter | solution.py:87
  116.9 6.9 %copy-start.1 = (f32[6,224,1536]{2,1,0:T(8,128)S(1)}, f32[6,224,1536]{2,1,0:T(8,128)}, u32[]{:S(2)}) copy-start(f32[6,224,1536]{2,1,0:T(8,128)} %get-tuple-element.17) | copy-start | bytes 24772612
  118.7 5.1 %copy-start.5 = (f32[6,224]{1,0:T(8,128)S(1)}, f32[6,224]{1,0:T(8,128)}, u32[]{:S(2)}) copy-start(f32[6,224]{1,0:T(8,128)} %copy-done.4) | copy-start | bytes 16132
  122.3 1.6 copy-start.7
  126.2 2.0 copy-start.2
  130.5 66.6 %reduce-scatter.5.cloned.1.call-start = ((), (), s32[]{:S(2)}) async-start(), calls=%async_computation.4 | async-start | bytes 1032192 | tf_op jit(solution)/shard_map/reduce_scatter | solution.py:99
  131.2 50.6 %copy-start.6 = (f32[6,224]{1,0:T(8,128)S(1)}, f32[6,224]{1,0:T(8,128)}, u32[]{:S(2)}) copy-start(f32[6,224]{1,0:T(8,128)} %copy-done.4) | copy-start | bytes 16132
  181.8 5.5 %copy-start.3 = (bf16[6,224,1536]{2,1,0:T(8,128)(2,1)S(1)}, bf16[6,224,1536]{2,1,0:T(8,128)(2,1)}, u32[]{:S(2)}) copy-start(bf16[6,224,1536]{2,1,0:T(8,128)(2,1)} %copy-done.2) | copy-start | bytes 12386308
Sparse Core Ops, SparseCore 0:
  59.3 57.5 all-reduce.1
  130.6 29.8 reduce-scatter.2
  164.8 32.2 reduce-scatter.4
where the time goes:
time: 206 us; the launch traced here: 205 us
  waiting for transfers between devices  93.5 us (45%)
  blocking collectives  55.2 us (27%)
  matrix products  24.5 us (12%)
  between operations  13.9 us (7%)
  other arithmetic  13.1 us (6%)
  local copies, waits for them, and re-layouts  4.87 us (2%)
    psum x1, waiting for transfers between devices, body(): context = lax.psum(value_partial, 'frame')  57.4 us
    reduce_scatter x1, waiting for transfers between devices, body(): lax.psum_scatter(jnp.einsum('slf,fd->lsd', score_gradient, upstream_signa...  28.7 us
    psum x1, blocking collectives, body(): loss = lax.psum(jnp.sum(loss_part), 'rec')  17.1 us
    all_gather x1, blocking collectives, body(): lax.all_gather(texts, 'rec', axis=0, tiled=True)  16.6 us
    all_gather x1, blocking collectives, body(): query_vectors = lax.all_gather(local, 'frame', axis=1, tiled=True)  12.4 us
    pmax x1, blocking collectives, body(): row_max = lax.pmax(local_max, 'frame')  9.08 us
    reduce_scatter x1, waiting for transfers between devices, body(): lax.psum_scatter(text_term, 'rec', scatter_dimension=0, tiled=True)  7.46 us
    dot_general x1, matrix products, body(): jnp.einsum('pqx,xh->pqh', batch_weights, upstream_signal, preferred_eleme...  5.96 us
  transfers between devices with their start and end apart: 3, of which 3 were waited for; matrix products, arithmetic and copies ran while one was open for 5% of the time, Pallas kernels for 0%

commit v1 on v0

--- a/solution.py
+++ b/solution.py
@@ -69,7 +69,7 @@
     query_f = query_vectors.astype(jnp.float32)
     q_norm = lax.rsqrt(jnp.sum(query_f * query_f, axis=2) + EPS)
     q_unit = query_f * q_norm[..., None]
-    context = lax.psum(value_partial, "frame")
+    context = jnp.sum(lax.all_gather(value_partial, "frame"), axis=0)
     c_norm = lax.rsqrt(jnp.sum(context * context, axis=2) + EPS)
     c_unit = context * c_norm[..., None]
     cos = jnp.sum(q_unit * c_unit, axis=2)

time: 206 us -> 213 us (1.034)
  waiting for transfers between devices: 93.5 us -> 99.5 us
  matrix products: 24.5 us -> 26.7 us
    all_gather x0 -> x1, waiting for transfers between devices: none -> 63.4 us  [body(): context = jnp.sum(lax.all_gather(value_partial, 'frame'), axis=0)]
    psum x1 -> x0, waiting for transfers between devices: 57.4 us -> none  [body(): context = lax.psum(value_partial, 'frame')]
    reduce_sum x0 -> x1, other arithmetic: none -> 3.1 us  [body(): context = jnp.sum(lax.all_gather(value_partial, 'frame'), axis=0)]
    dot_general x1, matrix products: 2.32 us -> 4.58 us  [body(): jnp.einsum('ype,je->ypj', context_batch_gradient, upstream_signal, prefer...]
  transfers between devices with their start and end apart: 3 -> 3, of which waited for: 3 -> 3; matrix products, arithmetic and copies ran while one was open for 5% -> 4% of each run, Pallas kernels for 0% -> 0%
where the time goes in v1:
time: 213 us
  waiting for transfers between devices  99.5 us (47%)
  blocking collectives  55.2 us (26%)
  matrix products  26.7 us (13%)
  between operations  14 us (7%)
  other arithmetic  11.8 us (6%)
  local copies, waits for them, and re-layouts  5.28 us (2%)
    all_gather x1, waiting for transfers between devices, body(): context = jnp.sum(lax.all_gather(value_partial, 'frame'), axis=0)  63.4 us
    reduce_scatter x1, waiting for transfers between devices, body(): lax.psum_scatter(jnp.einsum('slf,fd->lsd', score_gradient, upstream_signa...  28.6 us
    psum x1, blocking collectives, body(): loss = lax.psum(jnp.sum(loss_part), 'rec')  17.1 us
    all_gather x1, blocking collectives, body(): lax.all_gather(texts, 'rec', axis=0, tiled=True)  16.6 us
    all_gather x1, blocking collectives, body(): query_vectors = lax.all_gather(local, 'frame', axis=1, tiled=True)  12.4 us
    pmax x1, blocking collectives, body(): row_max = lax.pmax(local_max, 'frame')  9.08 us
    reduce_scatter x1, waiting for transfers between devices, body(): lax.psum_scatter(text_term, 'rec', scatter_dimension=0, tiled=True)  7.46 us
    dot_general x1, matrix products, body(): jnp.einsum('pqx,xh->pqh', batch_weights, upstream_signal, preferred_eleme...  5.92 us
  transfers between devices with their start and end apart: 3, of which 3 were waited for; matrix products, arithmetic and copies ran while one was open for 4% of the time, Pallas kernels for 0%

profile of v1, /device:TPU:0, one launch (start us, length us, event | category | flops | bytes accessed | tf_op | source)
XLA Modules:
  0.0 212.6 jit_solution(7416174934776923223)
XLA Ops:
  7.2 0.7 multiply_add_fusion
  8.6 0.9 select_reduce_fusion
  9.5 0.8 select_reduce_fusion.2
  10.4 16.6 %all_gather.12 = bf16[16,56,256]{2,1,0:T(8,128)(2,1)S(1)} all-gather(bf16[2,56,256]{2,1,0:T(8,128)(2,1)} %param.6), channel_id=1, replica_groups=mesh['rec'=8,'frame'=4] {'rec'}, dimensions={0}, use_global_device_ids=true | all-gather | bytes 516096 | tf_op jit(solution)/shard_map/all_gather | solution.py:50
  27.3 12.4 %all_gather.13 = bf16[6,224,256]{2,1,0:T(8,128)(2,1)S(1)} all-gather(bf16[6,56,256]{2,1,0:T(8,128)(2,1)S(1)} %copy.19), channel_id=1, replica_groups=mesh['rec'=8,'frame'=4] {'frame'}, dimensions={1}, use_global_device_ids=true | all-gather | bytes 860160 | tf_op jit(solution)/shard_map/all_gather | solution.py:53
  39.7 4.4 %multiply_reduce_fusion = (f32[6,224]{1,0:T(8,128)S(1)}, f32[6,224,1536]{2,1,0:T(8,128)}) fusion(bf16[6,224,256]{2,1,0:T(8,128)(2,1)S(1)} %all_gather.13, bf16[1,1536,256]{2,1,0:T(8,128)(2,1)S(1)} %copy-done), kind=kOutput, calls=%fused_computation.2 | convolution fusion | flops 1061092032 | bytes 9737472 | tf_op jit(solution)/shard_map/ype,je->ypj/dot_general | solution.py:57
  44.2 9.1 %pmax.7 = f32[6,224]{1,0:T(8,128)S(1)} all-reduce(f32[6,224]{1,0:T(8,128)S(1)} %get-tuple-element.16), channel_id=1, replica_groups=mesh['rec'=8,'frame'=4] {'frame'}, use_global_device_ids=true, to_apply=%region_6.0 | all-reduce | flops 1344 | bytes 10752 | tf_op jit(solution)/shard_map/pmax | solution.py:63
  53.3 5.9 %fusion.7 = f32[6,224,256]{2,1,0:T(8,128)} fusion(bf16[1,1536,256]{2,1,0:T(8,128)(2,1)S(1)} %copy-done, f32[6,224,1536]{2,1,0:T(8,128)} %get-tuple-element.17, f32[6,224]{1,0:T(8,128)S(1)} %pmax.7), kind=kOutput, calls=%fused_computation.18 | convolution fusion | flops 1063157760 | bytes 10425600 | tf_op jit(solution)/shard_map/pqx,xh->pqh/dot_general | solution.py:66
  59.6 63.4 %all-gather.3.cloned.1.call-done = f32[24,224,256]{2,1,0:T(8,128)} async-done(((f32[6,224,256]{2,1,0:T(8,128)}), f32[24,224,256]{2,1,0:T(8,128)}) %all-gather.3.cloned.1.call-update) | async-done | bytes 5505040 | tf_op jit(solution)/shard_map/all_gather | solution.py:72
  122.9 3.1 %reduce_sum.95 = f32[6,224,256]{2,1,0:T(8,128)S(1)} reduce(f32[4,6,224,256]{3,2,1,0:T(8,128)} %bitcast.43, f32[]{:T(128)} %constant.14.clone.1), dimensions={0}, to_apply=%region_7.0 | reduce | flops 1032192 | bytes 6881284 | tf_op jit(solution)/shard_map/reduce_sum | solution.py:72
  126.4 0.8 multiply_reduce_fusion.2
  127.1 0.7 fusion.31
  129.0 4.6 %multiply_convert_fusion = bf16[6,224,1536]{2,1,0:T(8,128)(2,1)S(1)} fusion(f32[6,224,1536]{2,1,0:T(8,128)} %get-tuple-element.17, bf16[6,224,256]{2,1,0:T(8,128)(2,1)S(1)} %get-tuple-element.13, f32[6,224]{1,0:T(8,128)S(1)} %copy-done.5, bf16[1,1536,256]{2,1,0:T(8,128)(2,1)S(1)} %copy-done), kind=kOutput, calls=%fused_computation | convolution fusion | flops 1067286528 | bytes 13866240 | tf_op jit(solution)/shard_map/ype,je->ypj/dot_general | solution.py:83
  133.6 2.0 copy-done.2
  135.6 2.3 %convolution_bitcast_fusion.2 = f32[224,6,256]{2,0,1:T(8,128)} fusion(bf16[6,224,1536]{2,1,0:T(8,128)(2,1)S(1)} %multiply_convert_fusion, bf16[1,1536,256]{2,1,0:T(8,128)(2,1)S(1)} %copy-done), kind=kOutput, calls=%fused_computation.11 | convolution fusion | flops 1056964608 | bytes 6291456 | tf_op jit(solution)/shard_map/slf,fd->lsd/dot_general | solution.py:88
  139.3 28.6 %reduce-scatter.3.cloned.1.call-done = f32[56,6,256]{2,0,1:T(8,128)} async-done(((f32[224,6,256]{2,0,1:T(8,128)}), f32[56,6,256]{2,0,1:T(8,128)}) %reduce-scatter.3.cloned.1.call-update) | async-done | bytes 344080 | tf_op jit(solution)/shard_map/reduce_scatter | solution.py:87
  168.0 1.2 fusion.19
  169.2 1.4 fusion.13
  170.6 1.5 copy.21
  172.1 17.1 %psum.7 = f32[]{:T(128)} all-reduce(f32[]{:T(128)} %get-tuple-element.15), channel_id=1, replica_groups=mesh['rec'=8,'frame'=4] {'rec'}, use_global_device_ids=true, to_apply=%region_11.12 | all-reduce | flops 1 | bytes 8 | tf_op jit(solution)/shard_map/psum | solution.py:109
  189.2 5.5 %convolution_bitcast_fusion = f32[1536,256]{1,0:T(8,128)S(1)} fusion(bf16[6,224,256]{2,1,0:T(8,128)(2,1)S(1)} %get-tuple-element.13, f32[6,224,1536]{2,1,0:T(8,128)} %get-tuple-element.17, f32[6,224]{1,0:T(8,128)S(1)} %copy-done.6), kind=kOutput, calls=%fused_computation.4 | convolution fusion | flops 1063157760 | bytes 10523904 | tf_op jit(solution)/shard_map/cvm,cvz->mz/dot_general | solution.py:105
  194.7 2.4 %fusion.3 = bf16[1,1536,256]{2,1,0:T(8,128)(2,1)} fusion(f32[1536,256]{1,0:T(8,128)S(1)} %convolution_bitcast_fusion, bf16[6,224,1536]{2,1,0:T(8,128)(2,1)S(1)} %copy-done.3, bf16[6,224,256]{2,1,0:T(8,128)(2,1)S(1)} %all_gather.13), kind=kOutput, calls=%fused_computation.8 | convolution fusion | flops 1057751040 | bytes 7176192 | tf_op jit(solution)/shard_map/cvm,cvz->mz/dot_general | solution.py:102
  197.1 7.5 %reduce-scatter.5.cloned.1.call-done = f32[2,56,256]{2,1,0:T(8,128)} async-done(((f32[16,56,256]{2,1,0:T(8,128)}), f32[2,56,256]{2,1,0:T(8,128)}) %reduce-scatter.5.cloned.1.call-update) | async-done | bytes 114704 | tf_op jit(solution)/shard_map/reduce_scatter | solution.py:99
  204.6 1.5 convert_element_type.54
  (36 shorter events, 4.2 us)
Async XLA Ops:
  7.2 32.6 %copy-start = (bf16[1,1536,256]{2,1,0:T(8,128)(2,1)S(1)}, bf16[1,1536,256]{2,1,0:T(8,128)(2,1)}, u32[]{:S(2)}) copy-start(bf16[1,1536,256]{2,1,0:T(8,128)(2,1)} %param.5) | copy-start | bytes 2359300
  7.2 115.8 %all-gather.3.cloned.1.call-start = ((), (), s32[]{:S(2)}) async-start(), calls=%async_computation.4 | async-start | bytes 6881280 | tf_op jit(solution)/shard_map/all_gather | solution.py:72
  10.3 16.9 %copy-start.8 = (s32[6]{0:T(128)}, s32[6]{0:T(128)S(1)}, u32[]{:S(2)}) copy-start(s32[6]{0:T(128)S(1)} %get-tuple-element.9) | copy-start | bytes 76
  10.4 16.9 %copy-start.9 = (pred[6]{0:T(512)(128)(4,1)}, pred[6]{0:T(512)(128)(4,1)S(1)}, u32[]{:S(2)}) copy-start(pred[6]{0:T(512)(128)(4,1)S(1)} %broadcast_compare_fusion) | copy-start | bytes 22
  53.2 5.9 %copy-start.4 = (f32[6,224]{1,0:T(8,128)}, f32[6,224]{1,0:T(8,128)S(1)}, u32[]{:S(2)}) copy-start(f32[6,224]{1,0:T(8,128)S(1)} %pmax.7) | copy-start | bytes 16132
  59.2 108.8 %reduce-scatter.3.cloned.1.call-start = ((), (), s32[]{:S(2)}) async-start(), calls=%async_computation.2 | async-start | bytes 1720320 | tf_op jit(solution)/shard_map/reduce_scatter | solution.py:87
  126.3 2.7 %copy-start.5 = (f32[6,224]{1,0:T(8,128)S(1)}, f32[6,224]{1,0:T(8,128)}, u32[]{:S(2)}) copy-start(f32[6,224]{1,0:T(8,128)} %copy-done.4) | copy-start | bytes 16132
  127.1 1.2 copy-start.1
  127.9 1.1 copy-start.7
  133.6 2.0 copy-start.2
  137.9 66.7 %reduce-scatter.5.cloned.1.call-start = ((), (), s32[]{:S(2)}) async-start(), calls=%async_computation.3 | async-start | bytes 1032192 | tf_op jit(solution)/shard_map/reduce_scatter | solution.py:99
  138.7 50.6 %copy-start.6 = (f32[6,224]{1,0:T(8,128)S(1)}, f32[6,224]{1,0:T(8,128)}, u32[]{:S(2)}) copy-start(f32[6,224]{1,0:T(8,128)} %copy-done.4) | copy-start | bytes 16132
  189.2 5.5 %copy-start.3 = (bf16[6,224,1536]{2,1,0:T(8,128)(2,1)S(1)}, bf16[6,224,1536]{2,1,0:T(8,128)(2,1)}, u32[]{:S(2)}) copy-start(bf16[6,224,1536]{2,1,0:T(8,128)(2,1)} %copy-done.2) | copy-start | bytes 12386308
Sparse Core Ops, SparseCore 0:
  59.3 63.5 all-gather.2
  138.1 29.8 reduce-scatter.2
  172.2 32.3 reduce-scatter.4
